TPU v7x, 32 devices: a whole 2x2x4 slice. The times are simulated.
32 devices in a mesh: dp: 8 (over z, y), tensor: 4 (over x, core).
Axes of the slice: x: 2, y: 2, z: 4, core: 2. Of those that a mesh axis runs over, the one named last changes fastest.
Arguments:
- tokens: bfloat16 [16384, 1024], P(('dp', 'tensor')), may hold values from -6 to 6
- ln_gain: float32 [1024], replicated, may hold values from 0.1 to 1.9
- ln_bias: float32 [1024], replicated, may hold values from -1.75 to 1.75
- w_qkv: bfloat16 [3, 1024, 16, 64], P(None, None, 'tensor'), may hold values from -0.1875 to 0.1875
- b_qkv: float32 [3, 16, 64], P(None, 'tensor'), may hold values from -3 to 3
- w_in: bfloat16 [1024, 4096], P(None, 'tensor'), may hold values from -0.1875 to 0.1875
- b_in: float32 [4096], P('tensor'), may hold values from -3 to 3
- w_out: bfloat16 [16, 64, 1024], P('tensor'), may hold values from -1.5 to 1.5
- w_down: bfloat16 [4096, 1024], P('tensor'), may hold values from -0.09375 to 0.09375
- b_out: float32 [1024], replicated, may hold values from -3 to 3
- cotangent: bfloat16 [16384, 1024], P(('dp', 'tensor')), may hold values from -6 to 6
- block_doc: int32 [8, 4], P('dp'), may hold values from 0 to 2, as said below
Outputs:
- block_out: bfloat16 [16384, 1024], P(('dp', 'tensor'))
- grad_tokens: float32 [16384, 1024], P(('dp', 'tensor'))
- grad_ln_gain: float32 [1024], replicated
- grad_ln_bias: float32 [1024], replicated
- grad_w_qkv: float32 [3, 1024, 16, 64], P(None, 'dp', 'tensor')
- grad_b_qkv: float32 [3, 16, 64], replicated
- grad_w_in: float32 [1024, 4096], P('dp', 'tensor')
- grad_b_in: float32 [4096], replicated
- grad_w_out: float32 [16, 64, 1024], P('tensor', None, 'dp')
- grad_w_down: float32 [4096, 1024], P('tensor', 'dp')
- grad_b_out: float32 [1024], replicated
Inputs may be any that keep to these rules, and one draw needn't show every extreme that they name: `block_doc`: in each group the numbers start at 0 and rise by 0 or 1 from block to block. Every sequence covers a power of two of blocks, at most 2; a sequence of k blocks starts at a block index divisible by k; each group has a sequence of exactly 2 blocks.
All inputs are finite; a program needn't handle non-finite values.
Results may differ from a plain program's by a relative error of at most 0.012.
The roundings to bfloat16 on the way count: a program that leaves them out, or rounds other values in their place, can miss the bound.
Values may be sent and summed in bfloat16 or wider, within the bound.
No kernel may reach another device: no remote copies, remote signals or barrier semaphores. Data moves between devices by JAX's collectives and lax.ppermute only.
A program may use at most 256 MiB of HBM per device.

v0:
```python
from functools import partial
import jax
import jax.numpy as jnp
from jax import lax
from jax.sharding import PartitionSpec as P

HEADS = 16
FF = 4096
ROT = 16
BLK = 512
epsilon = 1e-05


def layer_norm(rows, ln_gain, ln_bias):
    mean_row = jnp.mean(rows, axis=-1, keepdims=True)
    centred = rows - mean_row
    var_row = jnp.mean(centred * centred, axis=-1, keepdims=True)
    return centred * lax.rsqrt(var_row + epsilon) * ln_gain + ln_bias


def rope_tables(positions):
    half_dims = ROT // 2
    inverse = 1.0 / 10000.0 ** (jnp.arange(half_dims, dtype=jnp.float32) * 2.0 / ROT)
    angles = positions[:, None] * inverse[None, :]
    return (jnp.cos(angles), jnp.sin(angles))


def rotate(vectors, cosine_table, sine_table):
    half_dims = ROT // 2
    leading = vectors[..., :half_dims]
    trailing = vectors[..., half_dims:ROT]
    remain = vectors[..., ROT:]
    cosine = cosine_table[:, None, :]
    sine = sine_table[:, None, :]
    return jnp.concatenate(
        [leading * cosine - trailing * sine, trailing * cosine + leading * sine, remain], axis=-1
    )


def shards(
    tokens, ln_gain, ln_bias, w_qkv, b_qkv, w_in, b_in, w_out, w_down, b_out, cotangent, block_doc
):
    rows_local = tokens.shape[0]
    model_width = tokens.shape[1]
    heads_local = w_qkv.shape[2]
    head_dim = w_qkv.shape[3]
    attn_cols = heads_local * head_dim
    hidden_local = w_in.shape[1]
    score_scale = head_dim ** (-0.5)
    token_values = tokens.astype(jnp.float32)
    normed_rows, ln_back = jax.vjp(layer_norm, token_values, ln_gain, ln_bias)
    normed_low = normed_rows.astype(jnp.bfloat16)
    gathered = lax.all_gather(normed_low, "tensor", axis=0, tiled=True)
    group_rows = gathered.shape[0]
    num_blocks = group_rows // BLK
    seq_blocks = min(4, num_blocks // 2)
    window = seq_blocks * BLK
    pad_rows = window - BLK
    joined_weight = jnp.concatenate(
        [
            w_qkv[0].reshape(model_width, attn_cols),
            w_qkv[1].reshape(model_width, attn_cols),
            w_qkv[2].reshape(model_width, attn_cols),
            w_in,
        ],
        axis=1,
    )
    joined_bias = jnp.concatenate([b_qkv.reshape(3 * attn_cols), b_in])
    upward = jnp.dot(gathered, joined_weight, preferred_element_type=jnp.float32) + joined_bias
    query_pre = upward[:, :attn_cols].reshape(group_rows, heads_local, head_dim)
    key_pre = upward[:, attn_cols : 2 * attn_cols].reshape(group_rows, heads_local, head_dim)
    value_pre = upward[:, 2 * attn_cols : 3 * attn_cols].reshape(group_rows, heads_local, head_dim)
    hidden_pre = upward[:, 3 * attn_cols :]
    sequence_ids = block_doc[0]
    block_starts = jnp.sum(
        (sequence_ids[None, :] < sequence_ids[:, None]).astype(jnp.int32), axis=1
    )
    positions = (
        jnp.arange(group_rows, dtype=jnp.int32) - jnp.repeat(block_starts, BLK) * BLK
    ).astype(jnp.float32)
    cosine_table, sine_table = rope_tables(positions)
    all_queries = rotate(query_pre, cosine_table, sine_table).astype(jnp.bfloat16)
    all_keys = rotate(key_pre, cosine_table, sine_table).astype(jnp.bfloat16)
    all_values = value_pre.astype(jnp.bfloat16)
    pad_heads = jnp.zeros((pad_rows, heads_local, head_dim), jnp.bfloat16)
    keys_padded = jnp.concatenate([pad_heads, all_keys], axis=0)
    values_padded = jnp.concatenate([pad_heads, all_values], axis=0)
    padded_docs = jnp.concatenate([jnp.full((seq_blocks - 1,), -1, jnp.int32), sequence_ids])
    key_docs = jnp.repeat(padded_docs, BLK)
    query_offset = lax.broadcasted_iota(jnp.int32, (BLK, window), 0)
    key_offset = lax.broadcasted_iota(jnp.int32, (BLK, window), 1)
    causal = key_offset - pad_rows <= query_offset

    def window_scores(query_block):
        first_row = query_block * BLK
        query_rows = lax.dynamic_slice_in_dim(all_queries, first_row, BLK, 0)
        key_rows = lax.dynamic_slice_in_dim(keys_padded, first_row, window, 0)
        value_rows = lax.dynamic_slice_in_dim(values_padded, first_row, window, 0)
        window_docs = lax.dynamic_slice_in_dim(key_docs, first_row, window, 0)
        allowed = (window_docs[None, :] == sequence_ids[query_block]) & causal
        scores = (
            jnp.einsum("qhe,khe->hqk", query_rows, key_rows, preferred_element_type=jnp.float32)
            * score_scale
        )
        return (query_rows, key_rows, value_rows, jnp.where(allowed[None], scores, -1e30))

    def attend(query_block):
        query_rows, key_rows, value_rows, scores = window_scores(query_block)
        maxima = jnp.max(scores, axis=-1)
        log_total = maxima + jnp.log(jnp.sum(jnp.exp(scores - maxima[..., None]), axis=-1))
        weights = jax.nn.softmax(scores, axis=-1).astype(jnp.bfloat16)
        out_rows = jnp.einsum(
            "hqk,khe->qhe", weights, value_rows, preferred_element_type=jnp.float32
        )
        return (out_rows, log_total)

    attended_blocks, log_totals = lax.map(attend, jnp.arange(num_blocks, dtype=jnp.int32))
    attended = attended_blocks.reshape(group_rows, attn_cols).astype(jnp.bfloat16)
    w_out_flat = w_out.reshape(attn_cols, model_width)
    active_full, gelu_back = jax.vjp(partial(jax.nn.gelu, approximate=False), hidden_pre)
    active = active_full.astype(jnp.bfloat16)
    active_rows = lax.dynamic_slice_in_dim(
        active, jnp.int32(0), rows_local * lax.axis_size("tensor"), 0
    )
    mixed = lax.psum_scatter(
        jnp.dot(attended, w_out_flat, preferred_element_type=jnp.float32)
        + jnp.dot(active_rows, w_down, preferred_element_type=jnp.float32),
        "tensor",
        scatter_dimension=0,
        tiled=True,
    )
    block_out = (token_values + mixed + b_out).astype(jnp.bfloat16)
    cotangent_group = lax.all_gather(cotangent, "tensor", axis=0, tiled=True)
    grad_attended = jnp.einsum(
        "td,cd->tc", cotangent_group, w_out_flat, preferred_element_type=jnp.float32
    ).astype(jnp.bfloat16)
    grad_active = jnp.einsum(
        "td,fd->tf", cotangent_group, w_down, preferred_element_type=jnp.float32
    )
    grad_w_out = jnp.einsum(
        "tc,td->cd", attended, cotangent_group, preferred_element_type=jnp.float32
    )
    grad_w_down = jnp.einsum(
        "tf,td->fd", active, cotangent_group, preferred_element_type=jnp.float32
    )
    grad_hidden = gelu_back(grad_active)[0].astype(jnp.bfloat16)
    grad_out_heads = grad_attended.reshape(group_rows, heads_local, head_dim)

    def back_block(query_block, carried):
        grad_q_all, grad_k_padded, grad_v_padded = carried
        first_row = query_block * BLK
        query_rows, key_rows, value_rows, scores = window_scores(query_block)
        grad_rows_out = lax.dynamic_slice_in_dim(grad_out_heads, first_row, BLK, 0)
        weights = jnp.exp(scores - log_totals[query_block][..., None])
        grad_weights = jnp.einsum(
            "qhe,khe->hqk", grad_rows_out, value_rows, preferred_element_type=jnp.float32
        )
        deltas = jnp.sum(weights * grad_weights, axis=-1)
        grad_scores = (weights * (grad_weights - deltas[..., None])).astype(jnp.bfloat16)
        grad_q_rows = (
            jnp.einsum("hqk,khe->qhe", grad_scores, key_rows, preferred_element_type=jnp.float32)
            * score_scale
        )
        grad_k_rows = (
            jnp.einsum("hqk,qhe->khe", grad_scores, query_rows, preferred_element_type=jnp.float32)
            * score_scale
        )
        grad_v_rows = jnp.einsum(
            "hqk,qhe->khe",
            weights.astype(jnp.bfloat16),
            grad_rows_out,
            preferred_element_type=jnp.float32,
        )
        old_k = lax.dynamic_slice_in_dim(grad_k_padded, first_row, window, 0)
        old_v = lax.dynamic_slice_in_dim(grad_v_padded, first_row, window, 0)
        grad_k_padded = lax.dynamic_update_slice_in_dim(
            grad_k_padded, old_k + grad_k_rows, first_row, 0
        )
        grad_v_padded = lax.dynamic_update_slice_in_dim(
            grad_v_padded, old_v + grad_v_rows, first_row, 0
        )
        grad_q_all = lax.dynamic_update_slice_in_dim(grad_q_all, grad_q_rows, first_row, 0)
        return (grad_q_all, grad_k_padded, grad_v_padded)

    zero_heads = jnp.zeros((group_rows, heads_local, head_dim), jnp.float32)
    zero_padded = jnp.zeros((group_rows + pad_rows, heads_local, head_dim), jnp.float32)
    grad_queries, grad_k_padded, grad_v_padded = lax.fori_loop(
        0, num_blocks, back_block, (zero_heads, zero_padded, zero_padded)
    )
    grad_keys = grad_k_padded[pad_rows:]
    grad_values = grad_v_padded[pad_rows:]
    grad_q_pre = (
        rotate(grad_queries, cosine_table, -sine_table)
        .astype(jnp.bfloat16)
        .reshape(group_rows, attn_cols)
    )
    grad_k_pre = (
        rotate(grad_keys, cosine_table, -sine_table)
        .astype(jnp.bfloat16)
        .reshape(group_rows, attn_cols)
    )
    grad_v_pre = grad_values.astype(jnp.bfloat16).reshape(group_rows, attn_cols)
    grad_upward = jnp.concatenate([grad_q_pre, grad_k_pre, grad_v_pre, grad_hidden], axis=1)
    grad_joined_weight = jnp.einsum(
        "td,tc->dc", gathered, grad_upward, preferred_element_type=jnp.float32
    )
    grad_joined_bias = jnp.sum(grad_upward, axis=0, dtype=jnp.float32)
    grad_normed = lax.psum_scatter(
        jnp.einsum("tc,dc->td", grad_upward, joined_weight, preferred_element_type=jnp.float32),
        "tensor",
        scatter_dimension=0,
        tiled=True,
    )
    grad_tokens_norm, grad_gain_part, grad_bias_part = ln_back(grad_normed)
    grad_tokens = grad_tokens_norm + cotangent.astype(jnp.float32)
    grad_bout_part = jnp.sum(cotangent, axis=0, dtype=jnp.float32)
    grad_w_qkv_local = jnp.stack(
        [
            grad_joined_weight[:, member * attn_cols : (member + 1) * attn_cols].reshape(
                model_width, heads_local, head_dim
            )
            for member in range(3)
        ]
    )
    grad_w_in_local = grad_joined_weight[:, 3 * attn_cols :]
    tensor_rank = lax.axis_index("tensor")
    bqkv_full = lax.dynamic_update_slice(
        jnp.zeros((3, HEADS, head_dim), jnp.float32),
        grad_joined_bias[: 3 * attn_cols].reshape(3, heads_local, head_dim),
        (jnp.int32(0), tensor_rank * heads_local, jnp.int32(0)),
    )
    bin_full = lax.dynamic_update_slice(
        jnp.zeros((FF,), jnp.float32),
        grad_joined_bias[3 * attn_cols :],
        (tensor_rank * hidden_local,),
    )
    grad_ln_gain, grad_ln_bias, grad_b_out, grad_b_qkv, grad_b_in = lax.psum(
        (grad_gain_part, grad_bias_part, grad_bout_part, bqkv_full, bin_full), ("dp", "tensor")
    )
    grad_w_qkv, grad_w_in, grad_w_out_part, grad_w_down_part = (
        lax.psum_scatter(grad_w_qkv_local, "dp", scatter_dimension=1, tiled=True),
        lax.psum_scatter(grad_w_in_local, "dp", scatter_dimension=0, tiled=True),
        lax.psum_scatter(
            grad_w_out.reshape(heads_local, head_dim, model_width),
            "dp",
            scatter_dimension=2,
            tiled=True,
        ),
        lax.psum_scatter(grad_w_down, "dp", scatter_dimension=1, tiled=True),
    )
    return (
        block_out,
        grad_tokens,
        grad_ln_gain,
        grad_ln_bias,
        grad_w_qkv,
        grad_b_qkv,
        grad_w_in,
        grad_b_in,
        grad_w_out_part,
        grad_w_down_part,
        grad_b_out,
    )


def solution(mesh):
    return jax.shard_map(
        shards,
        mesh=mesh,
        in_specs=(
            P(("dp", "tensor"), None),
            P(),
            P(),
            P(None, None, "tensor", None),
            P(None, "tensor", None),
            P(None, "tensor"),
            P("tensor"),
            P("tensor", None, None),
            P("tensor", None),
            P(),
            P(("dp", "tensor"), None),
            P("dp", None),
        ),
        out_specs=(
            P(("dp", "tensor"), None),
            P(("dp", "tensor"), None),
            P(),
            P(),
            P(None, "dp", "tensor", None),
            P(),
            P("dp", "tensor"),
            P(),
            P("tensor", None, "dp"),
            P("tensor", "dp"),
            P(),
        ),
        check_vma=False,
    )
```

profile of v0, /device:TPU:0, one launch (start us, length us, event | category | flops | bytes accessed | tf_op | source)
XLA Modules:
  0.0 755.2 jit_solution(2105448763767745747)
XLA Ops:
  11.7 2.7 fusion.71
  22.3 29.4 %all-gather.3.cloned.1.call-done = bf16[2048,1024]{1,0:T(8,128)(2,1)} async-done(((bf16[512,1024]{1,0:T(8,128)(2,1)}), bf16[2048,1024]{1,0:T(8,128)(2,1)}) %all-gather.3.cloned.1.call-update) | async-done | bytes 4194320 | tf_op jit(solution)/shard_map/all_gather | solution.py:53
  51.7 14.2 %convolution_add_fusion = f32[2048,1792]{0,1:T(8,128)} fusion(bf16[2048,1024]{1,0:T(8,128)(2,1)} %all-gather.3.cloned.1.call-done, f32[1792]{0:T(1024)S(1)} %pad_maximum_fusion.8, bf16[1024,1024]{1,0:T(8,128)(2,1)} %param.21, bf16[1024,256]{1,0:T(8,128)(2,1)S(1)} %copy.38, bf16[1024,256]{1,0:T(8,128)(2,1)} %copy.37, bf16[1024,256]{1,0:T(8,128)(2,1)} %copy.36), kind=kOutput, calls=%fused_computation.77 | convolution fusion | flops 7534542848 | bytes 22551552 | tf_op jit(solution)/shard_map/dot_general | solution.py:69
  65.9 2.5 fusion.88
  74.0 59.7 %while.31 = (s32[]{:T(128)}, bf16[4,512,4,64]{1,3,2,0:T(8,128)(2,1)}, f32[4,4,512]{2,1,0:T(4,128)}, s32[4]{0:T(128)S(1)}, bf16[2560,4,64]{0,2,1:T(8,128)(2,1)}, ...) while((s32[]{:T(128)}, ...), condition=%wide.region_6.7_spmd.clone, body=%wide.region_3.6_spmd.clone.sunk | while | flops 563084288 | bytes 29175080 | solution.py:117
  78.9 2.8 fusion.128
  84.7 4.3 fusion.130
  93.9 2.8 fusion.128
  99.6 4.3 fusion.130
  108.8 2.8 fusion.128
  114.5 4.3 fusion.130
  123.7 2.8 fusion.128
  129.5 4.3 fusion.130
  133.8 4.7 convolution_convert_fusion
  143.6 80.2 %while.32 = (s32[]{:T(128)}, f32[2048,4,64]{0,2,1:T(8,128)}, f32[2560,4,64]{0,2,1:T(8,128)}, f32[2560,4,64]{0,2,1:T(8,128)}, bf16[2560,4,64]{0,2,1:T(8,128)(2,1)...) while((s32[]{:T(128)}, f32[2048,4,64]{0,2,1:T(8,128)}, ...), condition=%wide.region_10.11_spmd.clone, body=%wide.region_8.10_spmd.clone.sunk | while | flops 1375599616 | bytes 97585616 | solution.py:187
  148.6 4.2 multiply_reduce_fusion.2
  152.8 2.4 multiply_convert_fusion.3
  159.4 4.5 fusion.143
  168.6 4.2 multiply_reduce_fusion.2
  172.8 2.4 multiply_convert_fusion.3
  179.4 4.5 fusion.143
  188.6 4.2 multiply_reduce_fusion.2
  192.8 2.4 multiply_convert_fusion.3
  199.3 4.5 fusion.143
  208.6 4.2 multiply_reduce_fusion.2
  219.3 4.5 fusion.143
  230.4 26.7 %add_convert_fusion = (bf16[2048,1024]{0,1:T(8,128)(2,1)S(1)}, f32[2048,1024]{0,1:T(8,128)}) fusion(f32[2048,1792]{0,1:T(8,128)} %convolution_add_fusion, bf16[2048,1024]{1,0:T(8,128)(2,1)S(1)} %copy-done.29, bf16[1024,1024]{1,0:T(8,128)(2,1)S(1)} %copy-done), kind=kOutput, calls=%fused_computation.61 | convolution fusion | flops 4445962240 | bytes 27262976 | tf_op jit(solution)/shard_map/td,fd->tf/dot_general | solution.py:137
  259.2 12.7 %fusion.79 = f32[2048,1024]{1,0:T(8,128)} fusion(bf16[1024,1024]{1,0:T(8,128)(2,1)} %param.21, bf16[1024,256]{1,0:T(8,128)(2,1)S(1)} %copy-done.17, bf16[1024,256]{1,0:T(8,128)(2,1)S(1)} %copy-done.15, bf16[1024,256]{1,0:T(8,128)(2,1)S(1)} %copy-done.14, bf16[2048,1024]{0,1:T(8,128)(2,1)S(1)} %get-tuple-element.373, bf16[2048,256]{0,1:T(8,128)(2,1)S(1)} %bitcast.104, ...), kind=kOutput, calls=%fused_computation.119 | convolution fusion | flops 7560232960 | bytes 19398656 | tf_op jit(solution)/shard_map/tc,dc->td/dot_general | solution.py:209
  274.4 11.8 %multiply_convert_fusion.1 = bf16[2048,1024]{0,1:T(8,128)(2,1)} fusion(f32[2048,1024]{0,1:T(8,128)} %get-tuple-element.374, f32[2048,1792]{0,1:T(8,128)} %convolution_add_fusion), kind=kLoop, calls=%fused_computation.62 | loop fusion | flops 6291456 | bytes 20971520 | tf_op jit(solution)/shard_map/convert_element_type | solution.py:121
  286.2 6.6 fusion.91
  292.8 4.8 convolution_add_fusion.1
  297.7 4.4 fusion.59
  302.4 12.4 %fusion.85 = f32[1024,1792]{1,0:T(8,128)S(1)} fusion(bf16[2048,1024]{1,0:T(8,128)(2,1)} %all-gather.3.cloned.1.call-done, bf16[2048,1024]{0,1:T(8,128)(2,1)} %copy-done.6, bf16[2048,256]{0,1:T(8,128)(2,1)} %bitcast.105, bf16[2048,256]{0,1:T(8,128)(2,1)} %bitcast.114, bf16[2048,256]{0,1:T(8,128)(2,1)} %bitcast.111), kind=kOutput, calls=%fused_computation.149 | convolution fusion | flops 7545552896 | bytes 18874368 | tf_op jit(solution)/shard_map/td,tc->dc/dot_general | solution.py:204
  314.7 3.0 copy-done.5
  321.0 2.7 copy.41
  323.7 2.6 copy.42
  326.3 3.6 pad_maximum_fusion.2
  330.0 4.8 slice.139
  335.1 10.1 %fusion.92 = f32[1024,1024]{1,0:T(8,128)} fusion(bf16[2048,1024]{0,1:T(8,128)(2,1)} %multiply_convert_fusion.1, bf16[2048,1024]{1,0:T(8,128)(2,1)} %all-gather.5.cloned.1.call-done), kind=kOutput, calls=%fused_computation.155 | convolution fusion | flops 4294967296 | bytes 12582912 | tf_op jit(solution)/shard_map/tf,td->fd/dot_general | solution.py:143
  345.2 4.3 convert_reduce_fusion
  351.9 2.6 fusion.72
  354.4 63.1 %reduce-scatter.7.cloned.1.call-done = f32[512,1024]{1,0:T(8,128)} async-done(((f32[2048,1024]{1,0:T(8,128)}), f32[512,1024]{1,0:T(8,128)}) %reduce-scatter.7.cloned.1.call-update) | async-done | bytes 2097168 | tf_op jit(solution)/shard_map/reduce_scatter | solution.py:125
  417.5 5.1 convert_reduce_fusion.2
  422.7 40.9 %all-reduce.2 = (f32[1024]{0:T(1024)}, f32[1024]{0:T(1024)}, f32[3,16,64]{2,1,0:T(8,128)}, f32[4096]{0:T(1024)}, f32[1024]{0:T(1024)}) all-reduce(f32[1024]{0:T(1024)S(1)} %get-tuple-element.320, f32[1024]{0:T(1024)S(1)} %get-tuple-element.322, ...), channel_id=1, replica_groups=mesh['dp'=8,'tensor'=4] {'dp','tensor'}, use_global_device_ids=true, to_apply=%region_15.16 | all-reduce | flops 10240 | bytes 81920 | tf_op jit(solution)/shard_map/psum | solution.py:237
  463.6 22.5 %reduce-scatter.15.cloned.1.call-done = f32[4,64,128]{2,1,0:T(8,128)} async-done(((f32[4,64,1024]{2,1,0:T(8,128)}), f32[4,64,128]{2,1,0:T(8,128)}) %reduce-scatter.15.cloned.1.call-update) | async-done | bytes 131088 | tf_op jit(solution)/shard_map/reduce_scatter | solution.py:243
  486.1 77.8 %reduce-scatter.11.cloned.1.call-done = f32[3,128,4,64]{1,3,2,0:T(8,128)} async-done(((f32[3,1024,4,64]{1,3,2,0:T(8,128)}), f32[3,128,4,64]{1,3,2,0:T(8,128)}) %reduce-scatter.11.cloned.1.call-update) | async-done | bytes 393232 | tf_op jit(solution)/shard_map/reduce_scatter | solution.py:241
  563.8 91.7 %reduce-scatter.13.cloned.1.call-done = f32[128,1024]{1,0:T(8,128)} async-done(((f32[1024,1024]{1,0:T(8,128)}), f32[128,1024]{1,0:T(8,128)}) %reduce-scatter.13.cloned.1.call-update) | async-done | bytes 524304 | tf_op jit(solution)/shard_map/reduce_scatter | solution.py:242
  655.5 92.6 %reduce-scatter.17.cloned.1.call-done = f32[1024,128]{1,0:T(8,128)} async-done(((f32[1024,1024]{1,0:T(8,128)}), f32[1024,128]{1,0:T(8,128)}) %reduce-scatter.17.cloned.1.call-update) | async-done | bytes 524304 | tf_op jit(solution)/shard_map/reduce_scatter | solution.py:249
  (210 shorter events, 99.2 us)
Async XLA Ops:
  7.2 223.1 %copy-start = (bf16[1024,1024]{1,0:T(8,128)(2,1)S(1)}, bf16[1024,1024]{1,0:T(8,128)(2,1)}, u32[]{:S(2)}) copy-start(bf16[1024,1024]{1,0:T(8,128)(2,1)} %param.24) | copy-start | bytes 6291460
  7.2 13.6 %copy-start.26 = (f32[3,4,64]{2,1,0:T(4,128)S(1)}, f32[3,4,64]{2,1,0:T(4,128)}, u32[]{:S(2)}) copy-start(f32[3,4,64]{2,1,0:T(4,128)} %param.20) | copy-start | bytes 9220
  7.2 13.7 %copy-start.30 = (s32[1,4]{1,0:T(1,128)S(1)}, s32[1,4]{1,0:T(1,128)}, u32[]{:S(2)}) copy-start(s32[1,4]{1,0:T(1,128)} %param.27) | copy-start | bytes 52
  7.2 14.1 %copy-start.28 = (f32[1024]{0:T(1024)S(1)}, f32[1024]{0:T(1024)}, u32[]{:S(2)}) copy-start(f32[1024]{0:T(1024)} %param.22) | copy-start | bytes 12292
  7.2 44.5 %all-gather.3.cloned.1.call-start = ((), (), s32[]{:S(2)}) async-start(), calls=%async_computation.6 | async-start | bytes 5242880 | tf_op jit(solution)/shard_map/all_gather | solution.py:53
  8.8 2.2 copy-start.19
  14.4 119.4 %all-gather.5.cloned.1.call-start = ((), (), s32[]{:S(2)}) async-start(), calls=%async_computation.8 | async-start | bytes 5242880 | tf_op jit(solution)/shard_map/all_gather | solution.py:133
  15.1 334.6 %reduce-scatter.9.cloned.1.call-start = ((), (), s32[]{:S(2)}) async-start(), calls=%async_computation.9 | async-start | bytes 10485760 | tf_op jit(solution)/shard_map/reduce_scatter | solution.py:208
  20.8 45.1 %copy-start.16 = (bf16[1024,256]{1,0:T(8,128)(2,1)}, bf16[1024,256]{1,0:T(8,128)(2,1)S(1)}, u32[]{:S(2)}) copy-start(bf16[1024,256]{1,0:T(8,128)(2,1)S(1)} %copy.38) | copy-start | bytes 1572868
  22.3 48.1 %copy-start.11 = (f32[2048,8]{0,1:T(8,128)}, f32[2048,8]{0,1:T(8,128)S(1)}, u32[]{:S(2)}) copy-start(f32[2048,8]{0,1:T(8,128)S(1)} %get-tuple-element.404) | copy-start | bytes 196612
  133.8 9.9 %copy-start.1 = (bf16[2560,4,64]{0,2,1:T(8,128)(2,1)S(1)}, bf16[2560,4,64]{0,2,1:T(8,128)(2,1)}, u32[]{:S(2)}) copy-start(bf16[2560,4,64]{0,2,1:T(8,128)(2,1)} %get-tuple-element.658) | copy-start | bytes 3932164
  143.6 83.4 %copy-start.12 = (f32[2048,8]{0,1:T(8,128)S(1)}, f32[2048,8]{0,1:T(8,128)}, u32[]{:S(2)}) copy-start(f32[2048,8]{0,1:T(8,128)} %copy-done.11) | copy-start | bytes 196612
  143.6 83.4 %copy-start.18 = (f32[2048,8]{0,1:T(8,128)S(1)}, f32[2048,8]{0,1:T(8,128)}, u32[]{:S(2)}) copy-start(f32[2048,8]{0,1:T(8,128)} %get-tuple-element.402) | copy-start | bytes 196612
  143.9 2.4 copy-start.31
  143.9 4.8 copy-start.10
  152.8 2.4 copy-start.3
  163.9 2.3 copy-start.31
  163.9 4.7 copy-start.10
  172.8 2.4 copy-start.3
  177.2 2.2 copy-start.4
  183.8 2.3 copy-start.31
  183.8 4.7 copy-start.10
  192.8 2.4 copy-start.3
  197.1 2.2 copy-start.4
  203.8 2.3 copy-start.31
  203.8 4.7 copy-start.10
  212.8 2.4 copy-start.3
  217.1 2.2 copy-start.4
  223.8 6.5 copy-start.29
  230.2 27.0 %copy-start.7 = (bf16[2048,4,64]{0,2,1:T(8,128)(2,1)}, bf16[2048,4,64]{0,2,1:T(8,128)(2,1)S(1)}, u32[]{:S(2)}) copy-start(bf16[2048,4,64]{0,2,1:T(8,128)(2,1)S(1)} %slice.174) | copy-start | bytes 3145732
  230.3 26.8 %copy-start.8 = (bf16[2048,4,64]{0,2,1:T(8,128)(2,1)}, bf16[2048,4,64]{0,2,1:T(8,128)(2,1)S(1)}, u32[]{:S(2)}) copy-start(bf16[2048,4,64]{0,2,1:T(8,128)(2,1)S(1)} %get-tuple-element.405) | copy-start | bytes 3145732
  230.4 26.8 %copy-start.9 = (bf16[2048,4,64]{0,2,1:T(8,128)(2,1)}, bf16[2048,4,64]{0,2,1:T(8,128)(2,1)S(1)}, u32[]{:S(2)}) copy-start(bf16[2048,4,64]{0,2,1:T(8,128)(2,1)S(1)} %get-tuple-element.406) | copy-start | bytes 3145732
  230.4 28.8 %copy-start.14 = (bf16[1024,256]{1,0:T(8,128)(2,1)S(1)}, bf16[1024,256]{1,0:T(8,128)(2,1)}, u32[]{:S(2)}) copy-start(bf16[1024,256]{1,0:T(8,128)(2,1)} %copy.36) | copy-start | bytes 1572868
  230.4 28.8 %copy-start.15 = (bf16[1024,256]{1,0:T(8,128)(2,1)S(1)}, bf16[1024,256]{1,0:T(8,128)(2,1)}, u32[]{:S(2)}) copy-start(bf16[1024,256]{1,0:T(8,128)(2,1)} %copy.37) | copy-start | bytes 1572868
  230.4 28.8 %copy-start.17 = (bf16[1024,256]{1,0:T(8,128)(2,1)S(1)}, bf16[1024,256]{1,0:T(8,128)(2,1)}, u32[]{:S(2)}) copy-start(bf16[1024,256]{1,0:T(8,128)(2,1)} %copy-done.16) | copy-start | bytes 1572868
  271.9 145.6 %reduce-scatter.7.cloned.1.call-start = ((), (), s32[]{:S(2)}) async-start(), calls=%async_computation.7 | async-start | bytes 10485760 | tf_op jit(solution)/shard_map/reduce_scatter | solution.py:125
  286.2 6.6 copy-start.13
  297.6 188.5 %reduce-scatter.15.cloned.1.call-start = ((), (), s32[]{:S(2)}) async-start(), calls=%async_computation.12 | async-start | bytes 1179648 | tf_op jit(solution)/shard_map/reduce_scatter | solution.py:243
  302.1 261.7 %reduce-scatter.11.cloned.1.call-start = ((), (), s32[]{:S(2)}) async-start(), calls=%async_computation.10 | async-start | bytes 3538944 | tf_op jit(solution)/shard_map/reduce_scatter | solution.py:241
  314.7 3.0 copy-start.5
  329.9 325.6 %reduce-scatter.13.cloned.1.call-start = ((), (), s32[]{:S(2)}) async-start(), calls=%async_computation.11 | async-start | bytes 4718592 | tf_op jit(solution)/shard_map/reduce_scatter | solution.py:242
  334.8 413.3 %reduce-scatter.17.cloned.1.call-start = ((), (), s32[]{:S(2)}) async-start(), calls=%async_computation.13 | async-start | bytes 4718592 | tf_op jit(solution)/shard_map/reduce_scatter | solution.py:249
  345.2 4.5 copy-start.2
  345.2 4.5 copy-start.20
  345.2 4.5 copy-start.21
  345.2 6.7 copy-start.25
  345.2 6.7 copy-start.23
  345.2 72.3 %copy-start.27 = (f32[1024]{0:T(1024)S(1)}, f32[1024]{0:T(1024)}, u32[]{:S(2)}) copy-start(f32[1024]{0:T(1024)} %param.25) | copy-start | bytes 12292
  (4 other events, 5.4 us)
Sparse Core Ops, SparseCore 0:
  14.5 37.1 all-gather.2
  53.3 34.5 all-gather.4
  272.0 71.5 reduce-scatter.8
  346.1 71.4 reduce-scatter.6
  421.3 64.6 reduce-scatter.14
  490.1 73.6 reduce-scatter.10
  568.0 87.4 reduce-scatter.12
  659.7 88.3 reduce-scatter.16
where the time goes:
time: 760 us; the launch traced here: 755 us
  waiting for transfers between devices  378 us (50%)
  matrix products  185 us (24%)
  other arithmetic  70.6 us (9%)
  local copies, waits for them, and re-layouts  53.6 us (7%)
  blocking collectives  40.9 us (5%)
  between operations  14.9 us (2%)
  loops' own time  10.9 us (1%)
    reduce_scatter x1, waiting for transfers between devices, shards(): lax.psum_scatter(grad_w_down, 'dp', scatter_dimension=1, tiled=True)  92.6 us
    reduce_scatter x1, waiting for transfers between devices, shards(): lax.psum_scatter(grad_w_in_local, 'dp', scatter_dimension=0, tiled=True)  91.7 us
    reduce_scatter x1, waiting for transfers between devices, shards(): lax.psum_scatter(grad_w_qkv_local, 'dp', scatter_dimension=1, tiled=True)  77.8 us
    reduce_scatter x1, waiting for transfers between devices, shards(): lax.psum_scatter(jnp.dot(attended, w_out_flat, preferred_element_type=jnp...  63.1 us
    psum x1, blocking collectives, shards(): lax.psum((grad_gain_part, grad_bias_part, grad_bout_part, bqkv_full, bin_...  40.9 us
    all_gather x1, waiting for transfers between devices, shards(): gathered = lax.all_gather(normed_low, 'tensor', axis=0, tiled=True)  29.4 us
    dot_general x1, matrix products, shards(): jnp.einsum('td,fd->tf', cotangent_group, w_down, preferred_element_type=j...  26.7 us
    reduce_scatter x1, waiting for transfers between devices, shards(): lax.psum_scatter(grad_w_out.reshape(heads_local, head_dim, model_width),...  22.5 us
  transfers between devices with their start and end apart: 8, of which 6 were waited for; matrix products, arithmetic and copies ran while one was open for 21% of the time, Pallas kernels for 0%

commit v1 on v0

--- a/solution.py
+++ b/solution.py
@@ -50,7 +50,15 @@
     token_values = tokens.astype(jnp.float32)
     normed_rows, ln_back = jax.vjp(layer_norm, token_values, ln_gain, ln_bias)
     normed_low = normed_rows.astype(jnp.bfloat16)
-    gathered = lax.all_gather(normed_low, "tensor", axis=0, tiled=True)
+    ways, here, step = (lax.axis_size("tensor"), lax.axis_index("tensor"), normed_low.shape[0])
+    line, have = (normed_low, 1)
+    while have < ways:
+        line = jnp.concatenate(
+            [line, lax.ppermute(line, "tensor", [(d, (d - have) % ways) for d in range(ways)])],
+            axis=0,
+        )
+        have = 2 * have
+    gathered = jnp.roll(line, here * step, axis=0)
     group_rows = gathered.shape[0]
     num_blocks = group_rows // BLK
     seq_blocks = min(4, num_blocks // 2)

time: 760 us -> 816 us (1.074)
  waiting for transfers between devices: 378 us -> 414 us
  local copies, waits for them, and re-layouts: 53.6 us -> 68.1 us
    ppermute x0 -> x2, waiting for transfers between devices: none -> 65.3 us  [shards(): lax.ppermute(line, 'tensor', [(d, (d - have) % ways) for d in range(ways)])]
    all_gather x1 -> x0, waiting for transfers between devices: 29.4 us -> none  [shards(): gathered = lax.all_gather(normed_low, 'tensor', axis=0, tiled=True)]
    unnamed x59 -> x69, local copies, waits for them, and re-layouts: 6.61 us -> 15.1 us
  transfers between devices with their start and end apart: 8 -> 9, of which waited for: 6 -> 7; matrix products, arithmetic and copies ran while one was open for 21% -> 22% of each run, Pallas kernels for 0% -> 0%
where the time goes in v1:
time: 816 us; the launch traced here: 811 us
  waiting for transfers between devices  414 us (51%)
  matrix products  185 us (23%)
  other arithmetic  73.5 us (9%)
  local copies, waits for them, and re-layouts  68.1 us (8%)
  blocking collectives  40.9 us (5%)
  between operations  14.9 us (2%)
  loops' own time  10.9 us (1%)
    reduce_scatter x1, waiting for transfers between devices, shards(): lax.psum_scatter(grad_w_down, 'dp', scatter_dimension=1, tiled=True)  92.5 us
    reduce_scatter x1, waiting for transfers between devices, shards(): lax.psum_scatter(grad_w_in_local, 'dp', scatter_dimension=0, tiled=True)  91.5 us
    reduce_scatter x1, waiting for transfers between devices, shards(): lax.psum_scatter(grad_w_qkv_local, 'dp', scatter_dimension=1, tiled=True)  78.1 us
    ppermute x2, waiting for transfers between devices, shards(): lax.ppermute(line, 'tensor', [(d, (d - have) % ways) for d in range(ways)])  65.3 us
    reduce_scatter x1, waiting for transfers between devices, shards(): lax.psum_scatter(jnp.dot(attended, w_out_flat, preferred_element_type=jnp...  63.7 us
    psum x1, blocking collectives, shards(): lax.psum((grad_gain_part, grad_bias_part, grad_bout_part, bqkv_full, bin_...  40.9 us
    dot_general x1, matrix products, shards(): jnp.einsum('td,fd->tf', cotangent_group, w_down, preferred_element_type=j...  26.7 us
    reduce_scatter x1, waiting for transfers between devices, shards(): lax.psum_scatter(grad_w_out.reshape(heads_local, head_dim, model_width),...  22.8 us
  transfers between devices with their start and end apart: 9, of which 7 were waited for; matrix products, arithmetic and copies ran while one was open for 22% of the time, Pallas kernels for 0%

profile of v1, /device:TPU:0, one launch (start us, length us, event | category | flops | bytes accessed | tf_op | source)
XLA Modules:
  0.0 811.0 jit_solution(9306469256474887805)
XLA Ops:
  11.1 2.7 constant_dynamic-update-slice_fusion.5
  16.3 19.0 %collective-permute-done = bf16[512,1024]{1,0:T(8,128)(2,1)} collective-permute-done((bf16[512,1024]{1,0:T(8,128)(2,1)S(1)}, bf16[512,1024]{1,0:T(8,128)(2,1)}, u32[]{:S(2)}, u32[]{:S(2)}) %collective-permute-start) | collective-permute-done | bytes 1048608 | tf_op jit(solution)/shard_map/ppermute | solution.py:57
  35.4 2.7 pad_maximum_fusion.3
  38.1 2.6 fusion.95
  50.8 46.3 %collective-permute-done.1 = bf16[1024,1024]{1,0:T(8,128)(2,1)} collective-permute-done((bf16[1024,1024]{1,0:T(8,128)(2,1)}, bf16[1024,1024]{1,0:T(8,128)(2,1)}, u32[]{:S(2)}, u32[]{:S(2)}) %collective-permute-start.1) | collective-permute-done | bytes 2097184 | tf_op jit(solution)/shard_map/ppermute | solution.py:57
  97.1 3.1 constant_dynamic-update-slice_fusion.3
  103.6 3.1 constant_dynamic-update-slice_fusion
  106.7 13.9 %convolution_add_fusion = f32[2048,1792]{0,1:T(8,128)} fusion(f32[1792]{0:T(1024)S(1)} %pad_maximum_fusion.9, bf16[4096,1024]{1,0:T(8,128)(2,1)} %constant_dynamic-update-slice_fusion, s32[]{:T(128)S(6)} %select_n.70, bf16[1024,1024]{1,0:T(8,128)(2,1)S(1)} %copy-done.32, bf16[1024,256]{1,0:T(8,128)(2,1)S(1)} %copy-done.18, ...), kind=kOutput, calls=%fused_computation.77 | convolution fusion | flops 7534542848 | bytes 22551556 | tf_op jit(solution)/shard_map/dot_general | solution.py:77
  128.7 59.7 %while.31 = (s32[]{:T(128)}, bf16[4,512,4,64]{1,3,2,0:T(8,128)(2,1)}, f32[4,4,512]{2,1,0:T(4,128)}, s32[4]{0:T(128)S(1)}, bf16[2560,4,64]{0,2,1:T(8,128)(2,1)}, ...) while((s32[]{:T(128)}, ...), condition=%wide.region_6.7_spmd.clone, body=%wide.region_3.6_spmd.clone.sunk | while | flops 563084288 | bytes 29175080 | solution.py:125
  133.6 2.8 fusion.131
  139.3 4.3 fusion.133
  148.5 2.8 fusion.131
  154.3 4.3 fusion.133
  163.4 2.8 fusion.131
  169.2 4.3 fusion.133
  178.4 2.8 fusion.131
  184.1 4.3 fusion.133
  188.4 4.7 convolution_convert_fusion
  198.2 80.2 %while.32 = (s32[]{:T(128)}, f32[2048,4,64]{0,2,1:T(8,128)}, f32[2560,4,64]{0,2,1:T(8,128)}, f32[2560,4,64]{0,2,1:T(8,128)}, bf16[2560,4,64]{0,2,1:T(8,128)(2,1)...) while((s32[]{:T(128)}, f32[2048,4,64]{0,2,1:T(8,128)}, ...), condition=%wide.region_10.11_spmd.clone, body=%wide.region_8.10_spmd.clone.sunk | while | flops 1375599616 | bytes 97585616 | solution.py:195
  203.2 4.2 multiply_reduce_fusion.2
  213.9 4.5 fusion.146
  223.2 4.2 multiply_reduce_fusion.2
  234.0 4.5 fusion.146
  243.2 4.2 multiply_reduce_fusion.2
  253.9 4.5 fusion.146
  263.2 4.2 multiply_reduce_fusion.2
  273.9 4.5 fusion.146
  285.0 26.7 %add_convert_fusion = (bf16[2048,1024]{0,1:T(8,128)(2,1)S(1)}, f32[2048,1024]{0,1:T(8,128)}) fusion(f32[2048,1792]{0,1:T(8,128)} %convolution_add_fusion, bf16[2048,1024]{1,0:T(8,128)(2,1)S(1)} %copy-done.31, bf16[1024,1024]{1,0:T(8,128)(2,1)S(1)} %copy-done), kind=kOutput, calls=%fused_computation.61 | convolution fusion | flops 4445962240 | bytes 27262976 | tf_op jit(solution)/shard_map/td,fd->tf/dot_general | solution.py:145
  313.9 12.7 %fusion.82 = f32[2048,1024]{1,0:T(8,128)} fusion(bf16[1024,1024]{1,0:T(8,128)(2,1)} %param.21, bf16[1024,256]{1,0:T(8,128)(2,1)S(1)} %copy-done.19, bf16[1024,256]{1,0:T(8,128)(2,1)S(1)} %copy-done.17, bf16[1024,256]{1,0:T(8,128)(2,1)S(1)} %copy-done.15, bf16[2048,1024]{0,1:T(8,128)(2,1)S(1)} %get-tuple-element.373, bf16[2048,256]{0,1:T(8,128)(2,1)S(1)} %bitcast.102, ...), kind=kOutput, calls=%fused_computation.123 | convolution fusion | flops 7560232960 | bytes 19398656 | tf_op jit(solution)/shard_map/tc,dc->td/dot_general | solution.py:217
  329.2 11.6 %multiply_convert_fusion.1 = bf16[2048,1024]{0,1:T(8,128)(2,1)} fusion(f32[2048,1024]{0,1:T(8,128)} %get-tuple-element.374, f32[2048,1792]{0,1:T(8,128)} %convolution_add_fusion), kind=kLoop, calls=%fused_computation.62 | loop fusion | flops 6291456 | bytes 20971520 | tf_op jit(solution)/shard_map/convert_element_type | solution.py:129
  340.8 6.6 fusion.96
  347.4 4.8 convolution_add_fusion.1
  352.3 4.4 fusion.59
  357.0 12.4 %fusion.61 = f32[1024,1792]{1,0:T(8,128)S(1)} fusion(bf16[4096,1024]{1,0:T(8,128)(2,1)} %constant_dynamic-update-slice_fusion, s32[]{:T(128)S(6)} %select_n.70, bf16[2048,1024]{0,1:T(8,128)(2,1)} %copy-done.6, bf16[2048,256]{0,1:T(8,128)(2,1)} %bitcast.103, bf16[2048,256]{0,1:T(8,128)(2,1)} %bitcast.112, bf16[2048,256]{0,1:T(8,128)(2,1)} %bitcast.109), kind=kOutput, calls=%fused_computation.82 | convolution fusion | flops 7545552896 | bytes 18874372 | tf_op jit(solution)/shard_map/td,tc->dc/dot_general | solution.py:212
  369.4 3.0 copy-done.5
  375.7 2.7 copy.41
  380.9 3.5 pad_maximum_fusion.2
  384.6 4.7 slice.139
  389.6 10.0 %fusion.97 = f32[1024,1024]{1,0:T(8,128)} fusion(bf16[2048,1024]{0,1:T(8,128)(2,1)} %multiply_convert_fusion.1, bf16[2048,1024]{1,0:T(8,128)(2,1)} %all-gather.2.cloned.1.call-done), kind=kOutput, calls=%fused_computation.166 | convolution fusion | flops 4294967296 | bytes 12582912 | tf_op jit(solution)/shard_map/tf,td->fd/dot_general | solution.py:151
  399.7 4.3 convert_reduce_fusion
  406.3 2.9 fusion.75
  409.2 63.7 %reduce-scatter.7.cloned.1.call-done = f32[512,1024]{1,0:T(8,128)} async-done(((f32[2048,1024]{1,0:T(8,128)}), f32[512,1024]{1,0:T(8,128)}) %reduce-scatter.7.cloned.1.call-update) | async-done | bytes 2097168 | tf_op jit(solution)/shard_map/reduce_scatter | solution.py:133
  472.9 5.1 convert_reduce_fusion.2
  478.0 40.9 %all-reduce.2 = (f32[1024]{0:T(1024)}, f32[1024]{0:T(1024)}, f32[3,16,64]{2,1,0:T(8,128)}, f32[4096]{0:T(1024)}, f32[1024]{0:T(1024)}) all-reduce(f32[1024]{0:T(1024)S(1)} %get-tuple-element.320, f32[1024]{0:T(1024)S(1)} %get-tuple-element.322, ...), channel_id=1, replica_groups=mesh['dp'=8,'tensor'=4] {'dp','tensor'}, use_global_device_ids=true, to_apply=%region_15.16 | all-reduce | flops 10240 | bytes 81920 | tf_op jit(solution)/shard_map/psum | solution.py:245
  519.0 22.8 %reduce-scatter.15.cloned.1.call-done = f32[4,64,128]{2,1,0:T(8,128)} async-done(((f32[4,64,1024]{2,1,0:T(8,128)}), f32[4,64,128]{2,1,0:T(8,128)}) %reduce-scatter.15.cloned.1.call-update) | async-done | bytes 131088 | tf_op jit(solution)/shard_map/reduce_scatter | solution.py:251
  541.8 78.1 %reduce-scatter.11.cloned.1.call-done = f32[3,128,4,64]{1,3,2,0:T(8,128)} async-done(((f32[3,1024,4,64]{1,3,2,0:T(8,128)}), f32[3,128,4,64]{1,3,2,0:T(8,128)}) %reduce-scatter.11.cloned.1.call-update) | async-done | bytes 393232 | tf_op jit(solution)/shard_map/reduce_scatter | solution.py:249
  619.8 91.5 %reduce-scatter.13.cloned.1.call-done = f32[128,1024]{1,0:T(8,128)} async-done(((f32[1024,1024]{1,0:T(8,128)}), f32[128,1024]{1,0:T(8,128)}) %reduce-scatter.13.cloned.1.call-update) | async-done | bytes 524304 | tf_op jit(solution)/shard_map/reduce_scatter | solution.py:250
  711.3 92.5 %reduce-scatter.17.cloned.1.call-done = f32[1024,128]{1,0:T(8,128)} async-done(((f32[1024,1024]{1,0:T(8,128)}), f32[1024,128]{1,0:T(8,128)}) %reduce-scatter.17.cloned.1.call-update) | async-done | bytes 524304 | tf_op jit(solution)/shard_map/reduce_scatter | solution.py:257
  (223 shorter events, 118.7 us)
Async XLA Ops:
  7.2 277.7 %copy-start = (bf16[1024,1024]{1,0:T(8,128)(2,1)S(1)}, bf16[1024,1024]{1,0:T(8,128)(2,1)}, u32[]{:S(2)}) copy-start(bf16[1024,1024]{1,0:T(8,128)(2,1)} %param.24) | copy-start | bytes 6291460
  7.2 181.2 %all-gather.2.cloned.1.call-start = ((), (), s32[]{:S(2)}) async-start(), calls=%async_computation.7 | async-start | bytes 5242880 | tf_op jit(solution)/shard_map/all_gather | solution.py:141
  8.8 5.0 copy-start.21
  11.1 2.8 copy-start.24
  11.1 35.7 %copy-start.28 = (f32[3,4,64]{2,1,0:T(4,128)S(1)}, f32[3,4,64]{2,1,0:T(4,128)}, u32[]{:S(2)}) copy-start(f32[3,4,64]{2,1,0:T(4,128)} %param.20) | copy-start | bytes 9220
  11.1 35.8 %copy-start.33 = (s32[1,4]{1,0:T(1,128)S(1)}, s32[1,4]{1,0:T(1,128)}, u32[]{:S(2)}) copy-start(s32[1,4]{1,0:T(1,128)} %param.27) | copy-start | bytes 52
  11.1 36.2 %copy-start.30 = (f32[1024]{0:T(1024)S(1)}, f32[1024]{0:T(1024)}, u32[]{:S(2)}) copy-start(f32[1024]{0:T(1024)} %param.22) | copy-start | bytes 12292
  13.8 21.5 %collective-permute-start = (bf16[512,1024]{1,0:T(8,128)(2,1)S(1)}, bf16[512,1024]{1,0:T(8,128)(2,1)}, u32[]{:S(2)}, u32[]{:S(2)}) collective-permute-start(bf16[512,1024]{1,0:T(8,128)(2,1)S(1)} %get-tuple-element.376), channel_id=1, source_target_pairs={{0,3},{1,0},{2,1},{3,2},{4,7},{5,4},{6,5},{7,6},{8,11},{9,8},{10,9... | collective-permute-start | bytes 3145736 | tf_op jit(solution)/shard_map/ppermute | solution.py:57
  16.2 387.9 %reduce-scatter.9.cloned.1.call-start = ((), (), s32[]{:S(2)}) async-start(), calls=%async_computation.8 | async-start | bytes 10485760 | tf_op jit(solution)/shard_map/reduce_scatter | solution.py:216
  38.1 59.0 %collective-permute-start.1 = (bf16[1024,1024]{1,0:T(8,128)(2,1)}, bf16[1024,1024]{1,0:T(8,128)(2,1)}, u32[]{:S(2)}, u32[]{:S(2)}) collective-permute-start(bf16[1024,1024]{1,0:T(8,128)(2,1)} %pad_maximum_fusion.3), channel_id=1, source_target_pairs={{0,2},{1,3},{2,0},{3,1},{4,6},{5,7},{6,4},{7,5},{8,10},{9,11},{10,... | collective-permute-start | bytes 6291464 | tf_op jit(solution)/shard_map/ppermute | solution.py:57
  48.3 76.8 %copy-start.11 = (f32[2048,8]{0,1:T(8,128)}, f32[2048,8]{0,1:T(8,128)S(1)}, u32[]{:S(2)}) copy-start(f32[2048,8]{0,1:T(8,128)S(1)} %get-tuple-element.406) | copy-start | bytes 196612
  48.3 58.4 %copy-start.14 = (bf16[1024,256]{1,0:T(8,128)(2,1)S(1)}, bf16[1024,256]{1,0:T(8,128)(2,1)}, u32[]{:S(2)}) copy-start(bf16[1024,256]{1,0:T(8,128)(2,1)} %copy.36) | copy-start | bytes 1572868
  48.3 58.4 %copy-start.16 = (bf16[1024,256]{1,0:T(8,128)(2,1)S(1)}, bf16[1024,256]{1,0:T(8,128)(2,1)}, u32[]{:S(2)}) copy-start(bf16[1024,256]{1,0:T(8,128)(2,1)} %copy.37) | copy-start | bytes 1572868
  48.3 58.4 %copy-start.18 = (bf16[1024,256]{1,0:T(8,128)(2,1)S(1)}, bf16[1024,256]{1,0:T(8,128)(2,1)}, u32[]{:S(2)}) copy-start(bf16[1024,256]{1,0:T(8,128)(2,1)} %copy.38) | copy-start | bytes 1572868
  48.3 58.4 %copy-start.32 = (bf16[1024,1024]{1,0:T(8,128)(2,1)S(1)}, bf16[1024,1024]{1,0:T(8,128)(2,1)}, u32[]{:S(2)}) copy-start(bf16[1024,1024]{1,0:T(8,128)(2,1)} %param.21) | copy-start | bytes 6291460
  188.4 9.8 %copy-start.1 = (bf16[2560,4,64]{0,2,1:T(8,128)(2,1)S(1)}, bf16[2560,4,64]{0,2,1:T(8,128)(2,1)}, u32[]{:S(2)}) copy-start(bf16[2560,4,64]{0,2,1:T(8,128)(2,1)} %get-tuple-element.659) | copy-start | bytes 3932164
  198.2 83.4 %copy-start.12 = (f32[2048,8]{0,1:T(8,128)S(1)}, f32[2048,8]{0,1:T(8,128)}, u32[]{:S(2)}) copy-start(f32[2048,8]{0,1:T(8,128)} %copy-done.11) | copy-start | bytes 196612
  198.2 83.5 %copy-start.20 = (f32[2048,8]{0,1:T(8,128)S(1)}, f32[2048,8]{0,1:T(8,128)}, u32[]{:S(2)}) copy-start(f32[2048,8]{0,1:T(8,128)} %get-tuple-element.404) | copy-start | bytes 196612
  198.4 2.4 copy-start.34
  198.4 4.8 copy-start.10
  207.4 2.4 copy-start.3
  218.5 2.3 copy-start.34
  218.5 4.7 copy-start.10
  227.4 2.4 copy-start.3
  238.5 4.7 copy-start.10
  247.4 2.4 copy-start.3
  258.4 4.7 copy-start.10
  267.4 2.4 copy-start.3
  278.4 6.5 copy-start.31
  284.8 27.0 %copy-start.7 = (bf16[2048,4,64]{0,2,1:T(8,128)(2,1)}, bf16[2048,4,64]{0,2,1:T(8,128)(2,1)S(1)}, u32[]{:S(2)}) copy-start(bf16[2048,4,64]{0,2,1:T(8,128)(2,1)S(1)} %slice.174) | copy-start | bytes 3145732
  284.9 26.8 %copy-start.8 = (bf16[2048,4,64]{0,2,1:T(8,128)(2,1)}, bf16[2048,4,64]{0,2,1:T(8,128)(2,1)S(1)}, u32[]{:S(2)}) copy-start(bf16[2048,4,64]{0,2,1:T(8,128)(2,1)S(1)} %get-tuple-element.407) | copy-start | bytes 3145732
  285.0 26.8 %copy-start.9 = (bf16[2048,4,64]{0,2,1:T(8,128)(2,1)}, bf16[2048,4,64]{0,2,1:T(8,128)(2,1)S(1)}, u32[]{:S(2)}) copy-start(bf16[2048,4,64]{0,2,1:T(8,128)(2,1)S(1)} %get-tuple-element.408) | copy-start | bytes 3145732
  285.0 28.9 %copy-start.15 = (bf16[1024,256]{1,0:T(8,128)(2,1)S(1)}, bf16[1024,256]{1,0:T(8,128)(2,1)}, u32[]{:S(2)}) copy-start(bf16[1024,256]{1,0:T(8,128)(2,1)} %copy.36) | copy-start | bytes 1572868
  285.0 28.9 %copy-start.17 = (bf16[1024,256]{1,0:T(8,128)(2,1)S(1)}, bf16[1024,256]{1,0:T(8,128)(2,1)}, u32[]{:S(2)}) copy-start(bf16[1024,256]{1,0:T(8,128)(2,1)} %copy.37) | copy-start | bytes 1572868
  285.0 28.9 %copy-start.19 = (bf16[1024,256]{1,0:T(8,128)(2,1)S(1)}, bf16[1024,256]{1,0:T(8,128)(2,1)}, u32[]{:S(2)}) copy-start(bf16[1024,256]{1,0:T(8,128)(2,1)} %copy.38) | copy-start | bytes 1572868
  326.6 146.3 %reduce-scatter.7.cloned.1.call-start = ((), (), s32[]{:S(2)}) async-start(), calls=%async_computation.6 | async-start | bytes 10485760 | tf_op jit(solution)/shard_map/reduce_scatter | solution.py:133
  340.8 6.6 copy-start.13
  352.2 189.5 %reduce-scatter.15.cloned.1.call-start = ((), (), s32[]{:S(2)}) async-start(), calls=%async_computation.11 | async-start | bytes 1179648 | tf_op jit(solution)/shard_map/reduce_scatter | solution.py:251
  356.7 263.1 %reduce-scatter.11.cloned.1.call-start = ((), (), s32[]{:S(2)}) async-start(), calls=%async_computation.9 | async-start | bytes 3538944 | tf_op jit(solution)/shard_map/reduce_scatter | solution.py:249
  369.4 3.0 copy-start.5
  384.5 326.8 %reduce-scatter.13.cloned.1.call-start = ((), (), s32[]{:S(2)}) async-start(), calls=%async_computation.10 | async-start | bytes 4718592 | tf_op jit(solution)/shard_map/reduce_scatter | solution.py:250
  389.3 414.6 %reduce-scatter.17.cloned.1.call-start = ((), (), s32[]{:S(2)}) async-start(), calls=%async_computation.12 | async-start | bytes 4718592 | tf_op jit(solution)/shard_map/reduce_scatter | solution.py:257
  399.6 4.5 copy-start.2
  399.6 4.5 copy-start.22
  399.6 4.5 copy-start.23
  399.6 6.7 copy-start.27
  399.6 6.7 copy-start.25
  399.7 73.2 %copy-start.29 = (f32[1024]{0:T(1024)S(1)}, f32[1024]{0:T(1024)}, u32[]{:S(2)}) copy-start(f32[1024]{0:T(1024)} %param.25) | copy-start | bytes 12292
  (8 other events, 16.2 us)
Sparse Core Ops, SparseCore 0:
  16.4 47.4 all-gather.1
  326.7 72.0 reduce-scatter.8
  401.4 71.4 reduce-scatter.6
  476.7 64.9 reduce-scatter.14
  545.8 74.0 reduce-scatter.10
  623.9 87.3 reduce-scatter.12
  715.5 88.3 reduce-scatter.16
